TPU v7x, 32 devices: a whole 2x2x4 slice. The times are simulated.
32 devices in a mesh: groups: 2 (over y), feat: 4 (over z), layer: 2 (over x), tok: 2 (over core).
Axes of the slice: x: 2, y: 2, z: 4, core: 2. Of those that a mesh axis runs over, the one named last changes fastest.
Arguments:
- residual_in: float32 [256, 2, 1792], P('groups', 'tok', 'feat'), parts along dimension 0, may hold values from -6 to 6
- attn_scale: float32 [2, 256], P('layer', 'groups'), parts along dimension 1, may hold values from 0.4 to 2.5
- mlp_scale: float32 [2, 256], P('layer', 'groups'), parts along dimension 1, may hold values from 0.4 to 2.5
- patterns: bfloat16 [2, 8, 4, 64, 64], P('layer', None, 'groups'), parts along dimension 2, may hold values from 0.0029907227 to 0.059814453
- lengths: int32 [4], P('groups'), parts along dimension 0, may hold values from 16 to 64
- value_proj: bfloat16 [2, 2, 1792, 1024], P('layer', 'tok', None, 'feat'), may hold values from -0.09375 to 0.09375
- out_proj: bfloat16 [2, 4, 256, 2, 2, 1792], P('layer', None, None, None, 'tok', 'feat'), may hold values from -0.125 to 0.125
- enc_weight: bfloat16 [2, 2, 1792, 512], P('layer', 'tok', None, 'feat'), may hold values from -0.09375 to 0.09375
- enc_bias: float32 [2, 512], P('layer', 'feat'), may hold values from -3 to 3
- dec_weight: bfloat16 [2, 2, 512, 2, 1792], P('layer', None, None, 'tok', 'feat'), may hold values from -0.25 to 0.25
- errors: float32 [2, 256, 2, 1792], P('layer', 'groups', 'tok', 'feat'), parts along dimension 1, may hold values from -4 to 4
- clamp_mode: int32 [2, 16384], P('layer', 'feat'), may hold values from 0 to 2
- clamp_index: int32 [2, 16384], P('layer', 'feat'), may hold values from 0 to 63
- clamp_values: float32 [64], replicated, may hold values from 0.25 to 3
- active_blocks: int32 [2, 4], P('layer', 'feat'), may hold values from 0 to 31
Outputs:
- residual_out: float32 [2, 256, 2, 1792], P('layer', 'groups', 'tok', 'feat'), parts along dimension 1
- features: bfloat16 [2, 256, 512], P('layer', 'groups', 'feat'), parts along dimension 1
There are 2 independent parts, one for each index of `groups`. A program takes and returns all parts, laid end to end along the dimension named above; an argument that names none is the same for every part. Nothing has to cross between parts.
Inputs may be any that keep to these rules, and one draw needn't show every extreme that they name: `clamp_mode`: 0 leaves a feature free, 1 sets it to its table value, 2 multiplies it by its table value. `lengths`: positions at or past a prompt's length are padding.
All inputs are finite; a program needn't handle non-finite values.
Results may differ from a plain program's by a relative error of at most 0.018.
Values may be sent and summed in bfloat16 or wider, within the bound.
A program may use at most 64 MiB of HBM per device.

v0:
```python
import jax
import jax.numpy as jnp
from jax import lax
from jax.sharding import PartitionSpec as P


def passed_along(value, axis, steps):
    count = lax.axis_size(axis)
    initial, last = (max(0, -steps), min(count, count - steps))
    return lax.ppermute(value, axis, [(source, source + steps) for source in range(initial, last)])


def columns(normed_rows):
    return lax.all_gather(normed_rows, "feat", axis=1, tiled=True)


def halves(partial_sum):
    return lax.psum(partial_sum, "tok")


def pick_block(lookup_table, chosen, block_len):
    shaped = lookup_table.reshape(-1, block_len)
    return lax.dynamic_slice_in_dim(shaped, chosen, 1, 0)[0]


def local(
    residual_in,
    attn_scale,
    mlp_scale,
    patterns,
    lengths,
    value_proj,
    out_proj,
    enc_weight,
    enc_bias,
    dec_weight,
    errors,
    clamp_mode,
    clamp_index,
    clamp_values,
    active_blocks,
):
    layer_count = lax.axis_size("layer")
    my_layer = lax.axis_index("layer")
    my_range = lax.axis_index("feat")
    seq_len = patterns.shape[3]
    prompt_count = patterns.shape[2]
    head_dim = out_proj.shape[2]
    per_group = out_proj.shape[3]
    kv_cols = value_proj.shape[3]
    width_cols = residual_in.shape[2]
    block_len = enc_bias.shape[1]
    total_rows = residual_in.shape[0]
    split_count = 1
    block_rows = seq_len // split_count
    micro_count = prompt_count * split_count
    section_count = layer_count + micro_count - 1
    source_rows = residual_in[:, 0, :]
    error_rows = errors[0, :, 0, :]
    value_weight = value_proj[0, 0]
    out_weight = out_proj[0].reshape(-1, width_cols)
    enc_rows = enc_weight[0, 0]
    enc_shift = enc_bias[0]
    dec_rows = dec_weight[0, :, :, 0, :]
    chosen = active_blocks[0, 0]
    modes = pick_block(clamp_mode[0], chosen, block_len)
    table_pick = pick_block(clamp_index[0], chosen, block_len)
    table_ids = jnp.arange(clamp_values.shape[0], dtype=jnp.int32)
    levels = jnp.sum(
        jnp.where(table_pick[:, None] == table_ids[None, :], clamp_values[None, :], 0.0), axis=1
    )
    group_id = my_range * kv_cols // head_dim
    group_pat = lax.dynamic_slice_in_dim(patterns[0], group_id * per_group, per_group, 0)
    positions = jnp.arange(seq_len, dtype=jnp.int32)
    scale_attn = attn_scale[0]
    scale_mlp = mlp_scale[0]

    def add_heads(piece):
        return jnp.dot(piece, out_weight, preferred_element_type=jnp.float32)

    def add_writes(piece):
        return jnp.einsum("rf,tfc->trc", piece, dec_rows, preferred_element_type=jnp.float32)

    def section(step_num, carry):
        recv_rows, links, value_cache, kept_rows, kept_feats = carry
        micro_raw = step_num - my_layer
        is_live = (micro_raw >= 0) & (micro_raw < micro_count)
        micro_num = jnp.clip(micro_raw, 0, micro_count - 1)
        prompt_num = micro_num // split_count
        block_num = micro_num % split_count
        first_row = micro_num * block_rows
        first_pos = block_num * block_rows
        start_rows = lax.dynamic_slice_in_dim(source_rows, first_row, block_rows, 0)
        rows_in = jnp.where(my_layer == 0, start_rows, recv_rows)
        row_attn = lax.dynamic_slice_in_dim(scale_attn, first_row, block_rows, 0)
        normed = (rows_in * row_attn[:, None]).astype(jnp.bfloat16)
        values = halves(
            jnp.dot(columns(normed), value_weight, preferred_element_type=jnp.float32)
        ).astype(jnp.bfloat16)
        value_cache = values
        query_pos = first_pos + jnp.arange(block_rows, dtype=jnp.int32)
        prompt_len = lax.dynamic_index_in_dim(lengths, prompt_num, 0, keepdims=False)
        keep_keys = (positions[None, :] <= query_pos[:, None]) & (positions[None, :] < prompt_len)
        block_pat = lax.dynamic_slice(
            group_pat, (0, prompt_num, first_pos, 0), (per_group, 1, block_rows, seq_len)
        )[:, 0]
        block_pat = jnp.where(keep_keys[None], block_pat, jnp.zeros_like(block_pat))
        head_out = (
            jnp.einsum("uqk,kc->qcu", block_pat, value_cache, preferred_element_type=jnp.float32)
            .astype(jnp.bfloat16)
            .reshape(block_rows, -1)
        )
        attention = add_heads(lax.all_gather(head_out, "feat", axis=1, tiled=True))
        middle = rows_in + attention
        row_mlp = lax.dynamic_slice_in_dim(scale_mlp, first_row, block_rows, 0)
        normed_mlp = (middle * row_mlp[:, None]).astype(jnp.bfloat16)
        preact = (
            halves(jnp.dot(columns(normed_mlp), enc_rows, preferred_element_type=jnp.float32))
            + enc_shift
        )
        active = jnp.maximum(preact, 0.0)
        clamped = jnp.where(modes == 1, levels, jnp.where(modes == 2, active * levels, active))
        live_rows = query_pos < prompt_len
        block_feats = jnp.where(live_rows[:, None], clamped, 0.0).astype(jnp.bfloat16)
        writes = add_writes(lax.all_gather(block_feats, "feat", axis=1, tiled=True))
        error_block = lax.dynamic_slice_in_dim(error_rows, first_row, block_rows, 0)
        acc_in = jnp.where(my_layer == 0, jnp.zeros_like(links), links)
        running = acc_in + writes
        recon = lax.dynamic_index_in_dim(running, my_layer, 0, keepdims=False)
        rows_next = middle + recon + error_block
        recv_rows, links = passed_along((rows_next, running), "layer", 1)
        old_rows = lax.dynamic_slice_in_dim(kept_rows, first_row, block_rows, 0)
        kept_rows = lax.dynamic_update_slice_in_dim(
            kept_rows, jnp.where(is_live, rows_next, old_rows), first_row, 0
        )
        old_feats = lax.dynamic_slice_in_dim(kept_feats, first_row, block_rows, 0)
        kept_feats = lax.dynamic_update_slice_in_dim(
            kept_feats, jnp.where(is_live, block_feats, old_feats), first_row, 0
        )
        return (recv_rows, links, value_cache, kept_rows, kept_feats)

    link_start = jnp.zeros((layer_count, block_rows, width_cols), jnp.float32)
    initial = (
        jnp.zeros((block_rows, width_cols), jnp.float32),
        link_start,
        jnp.zeros((seq_len, kv_cols), jnp.bfloat16),
        jnp.zeros((total_rows, width_cols), jnp.float32),
        jnp.zeros((total_rows, block_len), jnp.bfloat16),
    )
    final = lax.fori_loop(0, section_count, section, initial)
    return (final[3][None, :, None, :], final[4][None])


def solution(mesh):
    return jax.shard_map(
        local,
        mesh=mesh,
        in_specs=(
            P("groups", "tok", "feat"),
            P("layer", "groups"),
            P("layer", "groups"),
            P("layer", None, "groups", None, None),
            P("groups"),
            P("layer", "tok", None, "feat"),
            P("layer", None, None, None, "tok", "feat"),
            P("layer", "tok", None, "feat"),
            P("layer", "feat"),
            P("layer", None, None, "tok", "feat"),
            P("layer", "groups", "tok", "feat"),
            P("layer", "feat"),
            P("layer", "feat"),
            P(),
            P("layer", "feat"),
        ),
        out_specs=(P("layer", "groups", "tok", "feat"), P("layer", "groups", "feat")),
        check_vma=False,
    )
```

profile of v0, /device:TPU:0, one launch (start us, length us, event | category | flops | bytes accessed | tf_op | source)
XLA Modules:
  0.0 265.3 jit_solution(8046609144955655287)
XLA Ops:
  0.7 0.9 copy-done
  2.2 0.7 fusion.19
  3.0 0.7 select_reduce_fusion
  3.7 6.1 %copy.43 = bf16[1,4,256,2,1,448]{5,3,2,1,4,0:T(2,128)(2,1)} copy(bf16[1,4,256,2,1,448]{2,5,4,3,1,0:T(8,128)(2,1)} %param.23) | data formatting | bytes 3670016 | tf_op args[6]
  9.9 3.5 %reshape_squeeze.9 = bf16[2048,448]{1,0:T(8,128)(2,1)S(1)} reshape(bf16[1,4,256,2,1,448]{5,3,2,1,4,0:T(2,128)(2,1)} %copy.43) | data formatting | bytes 3670016 | tf_op jit(solution)/shard_map/reshape;squeeze | solution.py:61
  13.5 0.8 copy.44
  14.4 0.7 broadcast.116
  15.1 0.7 broadcast_in_dim.131
  15.9 247.6 %while.23 = (s32[]{:T(128)}, f32[64,448]{1,0:T(8,128)S(1)}, f32[2,64,448]{2,1,0:T(8,128)}, f32[128,448]{1,0:T(8,128)}, bf16[128,128]{1,0:T(8,128)(2,1)S(1)}, /*i...) while((s32[]{:T(128)}, f32[64,448]{1,0:T(8,128)S(1)}, ...), condition=%wide.region_4.5_spmd.clone.clone, body=%wide.region_1.4_spmd.clone.clone.sunk | while | flops 268976448 | bytes 11732813 | solution.py:150
  16.1 15.7 %all-gather.6 = bf16[4,448,64]{1,2,0:T(8,128)(2,1)S(1)} all-gather(bf16[1,448,64]{1,2,0:T(8,128)(2,1)S(1)} %fusion.57), channel_id=1, replica_groups=mesh['groups'=2,'feat'=4,'layer'=2,'tok'=2] {'feat'}, dimensions={0}, use_global_device_ids=true | all-gather | bytes 286720 | tf_op jit(solution)/shard_map/while/body/eval_jaxpr/all_gather | solution.py:14
  31.9 0.3 reshape.85
  32.2 1.5 fusion.58
  33.7 3.6 %psum.34 = bf16[64,256]{1,0:T(8,128)(2,1)S(1)} all-reduce(f32[64,256]{1,0:T(8,128)S(1)} %fusion.58), channel_id=1, replica_groups=mesh['groups'=2,'feat'=4,'layer'=2,'tok'=2] {'tok'}, use_global_device_ids=true, to_apply=%region_2.2 | all-reduce | flops 16384 | bytes 98304 | tf_op jit(solution)/shard_map/while/body/eval_jaxpr/psum | solution.py:18
  37.3 0.7 dynamic_slice.163
  37.9 0.7 iota_compare_fusion.4
  38.9 16.6 %all_gather.48 = bf16[64,2048]{0,1:T(8,128)(2,1)S(1)} all-gather(bf16[64,512]{0,1:T(8,128)(2,1)S(1)} %bitcast.101), channel_id=1, replica_groups=mesh['groups'=2,'feat'=4,'layer'=2,'tok'=2] {'feat'}, dimensions={1}, use_global_device_ids=true | all-gather | bytes 327680 | tf_op jit(solution)/shard_map/while/body/eval_jaxpr/all_gather | solution.py:113
  55.6 0.5 convolution_add_fusion.2
  56.2 14.5 %all-gather.7 = bf16[4,448,64]{1,2,0:T(8,128)(2,1)S(1)} all-gather(bf16[1,448,64]{1,2,0:T(8,128)(2,1)S(1)} %fusion.61), channel_id=1, replica_groups=mesh['groups'=2,'feat'=4,'layer'=2,'tok'=2] {'feat'}, dimensions={0}, use_global_device_ids=true | all-gather | bytes 286720 | tf_op jit(solution)/shard_map/while/body/eval_jaxpr/all_gather | solution.py:14
  70.9 0.3 reshape.86
  71.2 1.2 fusion.62
  72.4 3.4 %psum.35 = f32[64,128]{1,0:T(8,128)S(1)} all-reduce(f32[64,128]{1,0:T(8,128)S(1)} %fusion.62), channel_id=1, replica_groups=mesh['groups'=2,'feat'=4,'layer'=2,'tok'=2] {'tok'}, use_global_device_ids=true, to_apply=%region_3.3 | all-reduce | flops 8192 | bytes 65536 | tf_op jit(solution)/shard_map/while/body/eval_jaxpr/psum | solution.py:18
  76.0 12.0 %all_gather.49 = bf16[64,512]{1,0:T(8,128)(2,1)S(1)} all-gather(bf16[64,128]{1,0:T(8,128)(2,1)S(1)} %get-tuple-element.762), channel_id=1, replica_groups=mesh['groups'=2,'feat'=4,'layer'=2,'tok'=2] {'feat'}, dimensions={1}, use_global_device_ids=true | all-gather | bytes 81920 | tf_op jit(solution)/shard_map/while/body/eval_jaxpr/all_gather | solution.py:125
  88.0 1.6 fusion.63
  89.5 4.1 %collective-permute-start.1 = (f32[2,64,448]{2,1,0:T(8,128)S(1)}, f32[2,64,448]{2,1,0:T(8,128)}, u32[]{:S(2)}, u32[]{:S(2)}) collective-permute-start(f32[2,64,448]{2,1,0:T(8,128)S(1)} %fusion.63), channel_id=1, source_target_pairs={{0,2},{1,3},{4,6},{5,7},{8,10},{9,11},{12,14},{13,15},{16,18},{17,... | collective-permute-start | bytes 688136 | tf_op jit(solution)/shard_map/while/body/eval_jaxpr/ppermute | solution.py:10
  93.7 1.6 select_dynamic-update-slice_fusion.5
  95.3 1.3 collective-permute-start
  96.6 3.0 %collective-permute-done = f32[64,448]{1,0:T(8,128)S(1)} collective-permute-done((f32[64,448]{1,0:T(8,128)S(1)}, f32[64,448]{1,0:T(8,128)S(1)}, u32[]{:S(2)}, u32[]{:S(2)}) %collective-permute-start) | collective-permute-done | bytes 114720 | tf_op jit(solution)/shard_map/while/body/eval_jaxpr/ppermute | solution.py:10
  99.8 14.3 %all-gather.6 = bf16[4,448,64]{1,2,0:T(8,128)(2,1)S(1)} all-gather(bf16[1,448,64]{1,2,0:T(8,128)(2,1)S(1)} %fusion.57), channel_id=1, replica_groups=mesh['groups'=2,'feat'=4,'layer'=2,'tok'=2] {'feat'}, dimensions={0}, use_global_device_ids=true | all-gather | bytes 286720 | tf_op jit(solution)/shard_map/while/body/eval_jaxpr/all_gather | solution.py:14
  114.3 0.3 reshape.85
  114.6 1.5 fusion.58
  116.1 3.6 %psum.34 = bf16[64,256]{1,0:T(8,128)(2,1)S(1)} all-reduce(f32[64,256]{1,0:T(8,128)S(1)} %fusion.58), channel_id=1, replica_groups=mesh['groups'=2,'feat'=4,'layer'=2,'tok'=2] {'tok'}, use_global_device_ids=true, to_apply=%region_2.2 | all-reduce | flops 16384 | bytes 98304 | tf_op jit(solution)/shard_map/while/body/eval_jaxpr/psum | solution.py:18
  119.7 0.7 dynamic_slice.163
  120.3 0.7 iota_compare_fusion.4
  121.3 16.2 %all_gather.48 = bf16[64,2048]{0,1:T(8,128)(2,1)S(1)} all-gather(bf16[64,512]{0,1:T(8,128)(2,1)S(1)} %bitcast.101), channel_id=1, replica_groups=mesh['groups'=2,'feat'=4,'layer'=2,'tok'=2] {'feat'}, dimensions={1}, use_global_device_ids=true | all-gather | bytes 327680 | tf_op jit(solution)/shard_map/while/body/eval_jaxpr/all_gather | solution.py:113
  137.6 0.5 convolution_add_fusion.2
  138.2 13.8 %all-gather.7 = bf16[4,448,64]{1,2,0:T(8,128)(2,1)S(1)} all-gather(bf16[1,448,64]{1,2,0:T(8,128)(2,1)S(1)} %fusion.61), channel_id=1, replica_groups=mesh['groups'=2,'feat'=4,'layer'=2,'tok'=2] {'feat'}, dimensions={0}, use_global_device_ids=true | all-gather | bytes 286720 | tf_op jit(solution)/shard_map/while/body/eval_jaxpr/all_gather | solution.py:14
  152.2 0.3 reshape.86
  152.5 1.2 fusion.62
  153.7 3.4 %psum.35 = f32[64,128]{1,0:T(8,128)S(1)} all-reduce(f32[64,128]{1,0:T(8,128)S(1)} %fusion.62), channel_id=1, replica_groups=mesh['groups'=2,'feat'=4,'layer'=2,'tok'=2] {'tok'}, use_global_device_ids=true, to_apply=%region_3.3 | all-reduce | flops 8192 | bytes 65536 | tf_op jit(solution)/shard_map/while/body/eval_jaxpr/psum | solution.py:18
  157.3 12.0 %all_gather.49 = bf16[64,512]{1,0:T(8,128)(2,1)S(1)} all-gather(bf16[64,128]{1,0:T(8,128)(2,1)S(1)} %get-tuple-element.762), channel_id=1, replica_groups=mesh['groups'=2,'feat'=4,'layer'=2,'tok'=2] {'feat'}, dimensions={1}, use_global_device_ids=true | all-gather | bytes 81920 | tf_op jit(solution)/shard_map/while/body/eval_jaxpr/all_gather | solution.py:125
  169.3 1.6 fusion.63
  170.8 5.0 %collective-permute-start.1 = (f32[2,64,448]{2,1,0:T(8,128)S(1)}, f32[2,64,448]{2,1,0:T(8,128)}, u32[]{:S(2)}, u32[]{:S(2)}) collective-permute-start(f32[2,64,448]{2,1,0:T(8,128)S(1)} %fusion.63), channel_id=1, source_target_pairs={{0,2},{1,3},{4,6},{5,7},{8,10},{9,11},{12,14},{13,15},{16,18},{17,... | collective-permute-start | bytes 688136 | tf_op jit(solution)/shard_map/while/body/eval_jaxpr/ppermute | solution.py:10
  175.9 1.7 select_dynamic-update-slice_fusion.5
  177.5 1.3 collective-permute-start
  178.8 3.0 %collective-permute-done = f32[64,448]{1,0:T(8,128)S(1)} collective-permute-done((f32[64,448]{1,0:T(8,128)S(1)}, f32[64,448]{1,0:T(8,128)S(1)}, u32[]{:S(2)}, u32[]{:S(2)}) %collective-permute-start) | collective-permute-done | bytes 114720 | tf_op jit(solution)/shard_map/while/body/eval_jaxpr/ppermute | solution.py:10
  182.0 13.8 %all-gather.6 = bf16[4,448,64]{1,2,0:T(8,128)(2,1)S(1)} all-gather(bf16[1,448,64]{1,2,0:T(8,128)(2,1)S(1)} %fusion.57), channel_id=1, replica_groups=mesh['groups'=2,'feat'=4,'layer'=2,'tok'=2] {'feat'}, dimensions={0}, use_global_device_ids=true | all-gather | bytes 286720 | tf_op jit(solution)/shard_map/while/body/eval_jaxpr/all_gather | solution.py:14
  196.0 0.3 reshape.85
  196.3 1.5 fusion.58
  197.7 3.6 %psum.34 = bf16[64,256]{1,0:T(8,128)(2,1)S(1)} all-reduce(f32[64,256]{1,0:T(8,128)S(1)} %fusion.58), channel_id=1, replica_groups=mesh['groups'=2,'feat'=4,'layer'=2,'tok'=2] {'tok'}, use_global_device_ids=true, to_apply=%region_2.2 | all-reduce | flops 16384 | bytes 98304 | tf_op jit(solution)/shard_map/while/body/eval_jaxpr/psum | solution.py:18
  201.4 0.7 dynamic_slice.163
  202.0 0.7 iota_compare_fusion.4
  203.0 16.1 %all_gather.48 = bf16[64,2048]{0,1:T(8,128)(2,1)S(1)} all-gather(bf16[64,512]{0,1:T(8,128)(2,1)S(1)} %bitcast.101), channel_id=1, replica_groups=mesh['groups'=2,'feat'=4,'layer'=2,'tok'=2] {'feat'}, dimensions={1}, use_global_device_ids=true | all-gather | bytes 327680 | tf_op jit(solution)/shard_map/while/body/eval_jaxpr/all_gather | solution.py:113
  219.1 0.5 convolution_add_fusion.2
  219.7 13.8 %all-gather.7 = bf16[4,448,64]{1,2,0:T(8,128)(2,1)S(1)} all-gather(bf16[1,448,64]{1,2,0:T(8,128)(2,1)S(1)} %fusion.61), channel_id=1, replica_groups=mesh['groups'=2,'feat'=4,'layer'=2,'tok'=2] {'feat'}, dimensions={0}, use_global_device_ids=true | all-gather | bytes 286720 | tf_op jit(solution)/shard_map/while/body/eval_jaxpr/all_gather | solution.py:14
  233.8 0.3 reshape.86
  234.0 1.2 fusion.62
  235.3 3.4 %psum.35 = f32[64,128]{1,0:T(8,128)S(1)} all-reduce(f32[64,128]{1,0:T(8,128)S(1)} %fusion.62), channel_id=1, replica_groups=mesh['groups'=2,'feat'=4,'layer'=2,'tok'=2] {'tok'}, use_global_device_ids=true, to_apply=%region_3.3 | all-reduce | flops 8192 | bytes 65536 | tf_op jit(solution)/shard_map/while/body/eval_jaxpr/psum | solution.py:18
  238.8 12.0 %all_gather.49 = bf16[64,512]{1,0:T(8,128)(2,1)S(1)} all-gather(bf16[64,128]{1,0:T(8,128)(2,1)S(1)} %get-tuple-element.762), channel_id=1, replica_groups=mesh['groups'=2,'feat'=4,'layer'=2,'tok'=2] {'feat'}, dimensions={1}, use_global_device_ids=true | all-gather | bytes 81920 | tf_op jit(solution)/shard_map/while/body/eval_jaxpr/all_gather | solution.py:125
  250.8 1.6 fusion.63
  252.4 5.1 %collective-permute-start.1 = (f32[2,64,448]{2,1,0:T(8,128)S(1)}, f32[2,64,448]{2,1,0:T(8,128)}, u32[]{:S(2)}, u32[]{:S(2)}) collective-permute-start(f32[2,64,448]{2,1,0:T(8,128)S(1)} %fusion.63), channel_id=1, source_target_pairs={{0,2},{1,3},{4,6},{5,7},{8,10},{9,11},{12,14},{13,15},{16,18},{17,... | collective-permute-start | bytes 688136 | tf_op jit(solution)/shard_map/while/body/eval_jaxpr/ppermute | solution.py:10
  257.5 1.7 select_dynamic-update-slice_fusion.5
  259.1 1.3 collective-permute-start
  260.4 3.0 %collective-permute-done = f32[64,448]{1,0:T(8,128)S(1)} collective-permute-done((f32[64,448]{1,0:T(8,128)S(1)}, f32[64,448]{1,0:T(8,128)S(1)}, u32[]{:S(2)}, u32[]{:S(2)}) %collective-permute-start) | collective-permute-done | bytes 114720 | tf_op jit(solution)/shard_map/while/body/eval_jaxpr/ppermute | solution.py:10
  263.5 1.8 copy.45
  (55 shorter events, 3.5 us)
Async XLA Ops:
  0.6 1.0 copy-start
  9.8 3.5 %copy-start.2 = (f32[128,1,448]{0,2,1:T(8,128)S(1)}, f32[128,1,448]{0,2,1:T(8,128)}, u32[]{:S(2)}) copy-start(f32[128,1,448]{0,2,1:T(8,128)} %param.17) | copy-start | bytes 688132
  9.8 3.7 %copy-start.3 = (f32[1,128,1,448]{1,3,2,0:T(8,128)S(1)}, f32[1,128,1,448]{1,3,2,0:T(8,128)}, u32[]{:S(2)}) copy-start(f32[1,128,1,448]{1,3,2,0:T(8,128)} %param.27) | copy-start | bytes 688132
  9.8 6.0 %copy-start.4 = (f32[1,128]{1,0:T(1,128)S(1)}, f32[1,128]{1,0:T(1,128)}, u32[]{:S(2)}) copy-start(f32[1,128]{1,0:T(1,128)} %param.25) | copy-start | bytes 1540
  9.8 6.0 %copy-start.5 = (f32[1,128]{1,0:T(1,128)S(1)}, f32[1,128]{1,0:T(1,128)}, u32[]{:S(2)}) copy-start(f32[1,128]{1,0:T(1,128)} %param.18) | copy-start | bytes 1540
  9.9 6.0 %copy-start.6 = (s32[2]{0:T(128)S(1)}, s32[2]{0:T(128)}, u32[]{:S(2)}) copy-start(s32[2]{0:T(128)} %param.21) | copy-start | bytes 28
  9.9 6.0 %copy-start.7 = (f32[1,128]{1,0:T(1,128)S(1)}, f32[1,128]{1,0:T(1,128)}, u32[]{:S(2)}) copy-start(f32[1,128]{1,0:T(1,128)} %param.19) | copy-start | bytes 1540
  89.5 10.1 %collective-permute-start.1 = (f32[2,64,448]{2,1,0:T(8,128)S(1)}, f32[2,64,448]{2,1,0:T(8,128)}, u32[]{:S(2)}, u32[]{:S(2)}) collective-permute-start(f32[2,64,448]{2,1,0:T(8,128)S(1)} %fusion.63), channel_id=1, source_target_pairs={{0,2},{1,3},{4,6},{5,7},{8,10},{9,11},{12,14},{13,15},{16,18},{17,... | collective-permute-start | bytes 688136 | tf_op jit(solution)/shard_map/while/body/eval_jaxpr/ppermute | solution.py:10
  95.3 4.3 %collective-permute-start = (f32[64,448]{1,0:T(8,128)S(1)}, f32[64,448]{1,0:T(8,128)S(1)}, u32[]{:S(2)}, u32[]{:S(2)}) collective-permute-start(f32[64,448]{1,0:T(8,128)S(1)} %get-tuple-element.763), channel_id=1, source_target_pairs={{0,2},{1,3},{4,6},{5,7},{8,10},{9,11},{12,14},{13,15},{16,18},{17,... | collective-permute-start | bytes 344072 | tf_op jit(solution)/shard_map/while/body/eval_jaxpr/ppermute | solution.py:10
  170.8 11.0 %collective-permute-start.1 = (f32[2,64,448]{2,1,0:T(8,128)S(1)}, f32[2,64,448]{2,1,0:T(8,128)}, u32[]{:S(2)}, u32[]{:S(2)}) collective-permute-start(f32[2,64,448]{2,1,0:T(8,128)S(1)} %fusion.63), channel_id=1, source_target_pairs={{0,2},{1,3},{4,6},{5,7},{8,10},{9,11},{12,14},{13,15},{16,18},{17,... | collective-permute-start | bytes 688136 | tf_op jit(solution)/shard_map/while/body/eval_jaxpr/ppermute | solution.py:10
  177.5 4.3 %collective-permute-start = (f32[64,448]{1,0:T(8,128)S(1)}, f32[64,448]{1,0:T(8,128)S(1)}, u32[]{:S(2)}, u32[]{:S(2)}) collective-permute-start(f32[64,448]{1,0:T(8,128)S(1)} %get-tuple-element.763), channel_id=1, source_target_pairs={{0,2},{1,3},{4,6},{5,7},{8,10},{9,11},{12,14},{13,15},{16,18},{17,... | collective-permute-start | bytes 344072 | tf_op jit(solution)/shard_map/while/body/eval_jaxpr/ppermute | solution.py:10
  252.4 11.1 %collective-permute-start.1 = (f32[2,64,448]{2,1,0:T(8,128)S(1)}, f32[2,64,448]{2,1,0:T(8,128)}, u32[]{:S(2)}, u32[]{:S(2)}) collective-permute-start(f32[2,64,448]{2,1,0:T(8,128)S(1)} %fusion.63), channel_id=1, source_target_pairs={{0,2},{1,3},{4,6},{5,7},{8,10},{9,11},{12,14},{13,15},{16,18},{17,... | collective-permute-start | bytes 688136 | tf_op jit(solution)/shard_map/while/body/eval_jaxpr/ppermute | solution.py:10
  259.1 4.3 %collective-permute-start = (f32[64,448]{1,0:T(8,128)S(1)}, f32[64,448]{1,0:T(8,128)S(1)}, u32[]{:S(2)}, u32[]{:S(2)}) collective-permute-start(f32[64,448]{1,0:T(8,128)S(1)} %get-tuple-element.763), channel_id=1, source_target_pairs={{0,2},{1,3},{4,6},{5,7},{8,10},{9,11},{12,14},{13,15},{16,18},{17,... | collective-permute-start | bytes 344072 | tf_op jit(solution)/shard_map/while/body/eval_jaxpr/ppermute | solution.py:10
  263.5 1.8 copy-start.1
where the time goes:
time: 266 us; the launch traced here: 265 us
  blocking collectives  192 us (72%)
  local copies, waits for them, and re-layouts  21.1 us (8%)
  starting transfers between devices  18.2 us (7%)
  matrix products  14.7 us (6%)
  waiting for transfers between devices  9.11 us (3%)
  other arithmetic  8.55 us (3%)
    all_gather x6, blocking collectives, columns(): return lax.all_gather(normed_rows, 'feat', axis=1, tiled=True)  85.9 us
    all_gather x3, blocking collectives, section(): attention = add_heads(lax.all_gather(head_out, 'feat', axis=1, tiled=True))  48.9 us
    all_gather x3, blocking collectives, section(): writes = add_writes(lax.all_gather(block_feats, 'feat', axis=1, tiled=True))  36 us
    psum x6, blocking collectives, halves(): return lax.psum(partial_sum, 'tok')  21.1 us
    ppermute x6, starting transfers between devices, passed_along(): lax.ppermute(value, axis, [(source, source + steps) for source in range(i...  18.2 us
    ppermute x6, waiting for transfers between devices, passed_along(): lax.ppermute(value, axis, [(source, source + steps) for source in range(i...  9.11 us
    unnamed x19, local copies, waits for them, and re-layouts  8.06 us
  transfers between devices with their start and end apart: 6, of which 3 were waited for; matrix products, arithmetic and copies ran while one was open for 2% of the time, Pallas kernels for 0%

commit v1 on v0

--- a/solution.py
+++ b/solution.py
@@ -122,7 +122,7 @@
         clamped = jnp.where(modes == 1, levels, jnp.where(modes == 2, active * levels, active))
         live_rows = query_pos < prompt_len
         block_feats = jnp.where(live_rows[:, None], clamped, 0.0).astype(jnp.bfloat16)
-        writes = add_writes(lax.all_gather(block_feats, "feat", axis=1, tiled=True))
+        writes = add_writes(jnp.concatenate(lax.all_gather(block_feats, "feat"), axis=1))
         error_block = lax.dynamic_slice_in_dim(error_rows, first_row, block_rows, 0)
         acc_in = jnp.where(my_layer == 0, jnp.zeros_like(links), links)
         running = acc_in + writes

time: 266 us -> 271 us (1.019)
  blocking collectives: 192 us -> 196 us
    all_gather x3, blocking collectives: 36 us -> 39.4 us  [section(): lax.all_gather(block_feats, 'feat')]
where the time goes in v1:
time: 271 us; the launch traced here: 270 us
  blocking collectives  196 us (72%)
  local copies, waits for them, and re-layouts  21.3 us (8%)
  starting transfers between devices  18.3 us (7%)
  matrix products  14.7 us (5%)
  waiting for transfers between devices  9.11 us (3%)
  other arithmetic  8.55 us (3%)
    all_gather x6, blocking collectives, columns(): return lax.all_gather(normed_rows, 'feat', axis=1, tiled=True)  88 us
    all_gather x3, blocking collectives, section(): attention = add_heads(lax.all_gather(head_out, 'feat', axis=1, tiled=True))  47.8 us
    all_gather x3, blocking collectives, section(): lax.all_gather(block_feats, 'feat')  39.4 us
    psum x6, blocking collectives, halves(): return lax.psum(partial_sum, 'tok')  21.1 us
    ppermute x6, starting transfers between devices, passed_along(): lax.ppermute(value, axis, [(source, source + steps) for source in range(i...  18.3 us
    ppermute x6, waiting for transfers between devices, passed_along(): lax.ppermute(value, axis, [(source, source + steps) for source in range(i...  9.11 us
    unnamed x19, local copies, waits for them, and re-layouts  8.06 us
  transfers between devices with their start and end apart: 6, of which 3 were waited for; matrix products, arithmetic and copies ran while one was open for 2% of the time, Pallas kernels for 0%

profile of v1, /device:TPU:0, one launch (start us, length us, event | category | flops | bytes accessed | tf_op | source)
XLA Modules:
  0.0 270.0 jit_solution(17759779088368684759)
XLA Ops:
  0.7 0.9 copy-done
  2.2 0.7 fusion.18
  3.0 0.7 select_reduce_fusion
  3.7 6.1 %copy.47 = bf16[1,4,256,2,1,448]{5,3,2,1,4,0:T(2,128)(2,1)} copy(bf16[1,4,256,2,1,448]{2,5,4,3,1,0:T(8,128)(2,1)} %param.23) | data formatting | bytes 3670016 | tf_op args[6]
  9.9 3.5 %reshape_squeeze.9 = bf16[2048,448]{1,0:T(8,128)(2,1)S(1)} reshape(bf16[1,4,256,2,1,448]{5,3,2,1,4,0:T(2,128)(2,1)} %copy.47) | data formatting | bytes 3670016 | tf_op jit(solution)/shard_map/reshape;squeeze | solution.py:61
  13.5 0.8 copy.48
  14.4 0.7 broadcast.116
  15.1 0.7 broadcast_in_dim.131
  15.9 252.4 %while.23 = (s32[]{:T(128)}, f32[64,448]{1,0:T(8,128)S(1)}, f32[2,64,448]{2,1,0:T(8,128)}, f32[128,448]{1,0:T(8,128)}, bf16[128,128]{1,0:T(8,128)(2,1)S(1)}, /*i...) while((s32[]{:T(128)}, f32[64,448]{1,0:T(8,128)S(1)}, ...), condition=%wide.region_4.5_spmd.clone.clone, body=%wide.region_1.4_spmd.clone.clone.sunk | while | flops 268976448 | bytes 11994957 | solution.py:150
  16.1 15.7 %all-gather.9 = bf16[4,448,64]{1,2,0:T(8,128)(2,1)S(1)} all-gather(bf16[1,448,64]{1,2,0:T(8,128)(2,1)S(1)} %fusion.57), channel_id=1, replica_groups=mesh['groups'=2,'feat'=4,'layer'=2,'tok'=2] {'feat'}, dimensions={0}, use_global_device_ids=true | all-gather | bytes 286720 | tf_op jit(solution)/shard_map/while/body/eval_jaxpr/all_gather | solution.py:14
  31.9 0.3 reshape.113
  32.2 1.5 fusion.58
  33.7 3.6 %psum.34 = bf16[64,256]{1,0:T(8,128)(2,1)S(1)} all-reduce(f32[64,256]{1,0:T(8,128)S(1)} %fusion.58), channel_id=1, replica_groups=mesh['groups'=2,'feat'=4,'layer'=2,'tok'=2] {'tok'}, use_global_device_ids=true, to_apply=%region_2.2 | all-reduce | flops 16384 | bytes 98304 | tf_op jit(solution)/shard_map/while/body/eval_jaxpr/psum | solution.py:18
  37.3 0.7 dynamic_slice.163
  37.9 0.7 iota_compare_fusion.4
  38.9 16.6 %all_gather.57 = bf16[64,2048]{0,1:T(8,128)(2,1)S(1)} all-gather(bf16[64,512]{0,1:T(8,128)(2,1)S(1)} %bitcast.104), channel_id=1, replica_groups=mesh['groups'=2,'feat'=4,'layer'=2,'tok'=2] {'feat'}, dimensions={1}, use_global_device_ids=true | all-gather | bytes 327680 | tf_op jit(solution)/shard_map/while/body/eval_jaxpr/all_gather | solution.py:113
  55.6 0.5 convolution_add_fusion.2
  56.2 14.5 %all-gather.10 = bf16[4,448,64]{1,2,0:T(8,128)(2,1)S(1)} all-gather(bf16[1,448,64]{1,2,0:T(8,128)(2,1)S(1)} %fusion.61), channel_id=1, replica_groups=mesh['groups'=2,'feat'=4,'layer'=2,'tok'=2] {'feat'}, dimensions={0}, use_global_device_ids=true | all-gather | bytes 286720 | tf_op jit(solution)/shard_map/while/body/eval_jaxpr/all_gather | solution.py:14
  70.9 0.3 reshape.114
  71.2 1.2 fusion.62
  72.4 3.4 %psum.35 = f32[64,128]{1,0:T(8,128)S(1)} all-reduce(f32[64,128]{1,0:T(8,128)S(1)} %fusion.62), channel_id=1, replica_groups=mesh['groups'=2,'feat'=4,'layer'=2,'tok'=2] {'tok'}, use_global_device_ids=true, to_apply=%region_3.3 | all-reduce | flops 8192 | bytes 65536 | tf_op jit(solution)/shard_map/while/body/eval_jaxpr/psum | solution.py:18
  76.0 13.1 %all-gather.11 = bf16[256,128]{1,0:T(8,128)(2,1)S(1)} all-gather(bf16[64,128]{1,0:T(8,128)(2,1)S(1)} %get-tuple-element.762), channel_id=2, replica_groups=mesh['groups'=2,'feat'=4,'layer'=2,'tok'=2] {'feat'}, dimensions={0}, use_global_device_ids=true | all-gather | bytes 81920 | tf_op jit(solution)/shard_map/while/body/eval_jaxpr/all_gather | solution.py:125
  89.2 1.6 fusion.63
  90.8 4.1 %collective-permute-start.1 = (f32[2,64,448]{2,1,0:T(8,128)S(1)}, f32[2,64,448]{2,1,0:T(8,128)}, u32[]{:S(2)}, u32[]{:S(2)}) collective-permute-start(f32[2,64,448]{2,1,0:T(8,128)S(1)} %fusion.63), channel_id=1, source_target_pairs={{0,2},{1,3},{4,6},{5,7},{8,10},{9,11},{12,14},{13,15},{16,18},{17,... | collective-permute-start | bytes 688136 | tf_op jit(solution)/shard_map/while/body/eval_jaxpr/ppermute | solution.py:10
  94.9 1.6 select_dynamic-update-slice_fusion.5
  96.5 1.3 collective-permute-start
  97.8 3.0 %collective-permute-done = f32[64,448]{1,0:T(8,128)S(1)} collective-permute-done((f32[64,448]{1,0:T(8,128)S(1)}, f32[64,448]{1,0:T(8,128)S(1)}, u32[]{:S(2)}, u32[]{:S(2)}) %collective-permute-start) | collective-permute-done | bytes 114720 | tf_op jit(solution)/shard_map/while/body/eval_jaxpr/ppermute | solution.py:10
  101.0 14.4 %all-gather.9 = bf16[4,448,64]{1,2,0:T(8,128)(2,1)S(1)} all-gather(bf16[1,448,64]{1,2,0:T(8,128)(2,1)S(1)} %fusion.57), channel_id=1, replica_groups=mesh['groups'=2,'feat'=4,'layer'=2,'tok'=2] {'feat'}, dimensions={0}, use_global_device_ids=true | all-gather | bytes 286720 | tf_op jit(solution)/shard_map/while/body/eval_jaxpr/all_gather | solution.py:14
  115.7 0.3 reshape.113
  116.0 1.4 fusion.58
  117.4 3.6 %psum.34 = bf16[64,256]{1,0:T(8,128)(2,1)S(1)} all-reduce(f32[64,256]{1,0:T(8,128)S(1)} %fusion.58), channel_id=1, replica_groups=mesh['groups'=2,'feat'=4,'layer'=2,'tok'=2] {'tok'}, use_global_device_ids=true, to_apply=%region_2.2 | all-reduce | flops 16384 | bytes 98304 | tf_op jit(solution)/shard_map/while/body/eval_jaxpr/psum | solution.py:18
  121.0 0.7 dynamic_slice.163
  121.7 0.7 iota_compare_fusion.4
  122.7 15.6 %all_gather.57 = bf16[64,2048]{0,1:T(8,128)(2,1)S(1)} all-gather(bf16[64,512]{0,1:T(8,128)(2,1)S(1)} %bitcast.104), channel_id=1, replica_groups=mesh['groups'=2,'feat'=4,'layer'=2,'tok'=2] {'feat'}, dimensions={1}, use_global_device_ids=true | all-gather | bytes 327680 | tf_op jit(solution)/shard_map/while/body/eval_jaxpr/all_gather | solution.py:113
  138.4 0.5 convolution_add_fusion.2
  138.9 14.5 %all-gather.10 = bf16[4,448,64]{1,2,0:T(8,128)(2,1)S(1)} all-gather(bf16[1,448,64]{1,2,0:T(8,128)(2,1)S(1)} %fusion.61), channel_id=1, replica_groups=mesh['groups'=2,'feat'=4,'layer'=2,'tok'=2] {'feat'}, dimensions={0}, use_global_device_ids=true | all-gather | bytes 286720 | tf_op jit(solution)/shard_map/while/body/eval_jaxpr/all_gather | solution.py:14
  153.6 0.3 reshape.114
  153.9 1.2 fusion.62
  155.1 3.4 %psum.35 = f32[64,128]{1,0:T(8,128)S(1)} all-reduce(f32[64,128]{1,0:T(8,128)S(1)} %fusion.62), channel_id=1, replica_groups=mesh['groups'=2,'feat'=4,'layer'=2,'tok'=2] {'tok'}, use_global_device_ids=true, to_apply=%region_3.3 | all-reduce | flops 8192 | bytes 65536 | tf_op jit(solution)/shard_map/while/body/eval_jaxpr/psum | solution.py:18
  158.6 13.1 %all-gather.11 = bf16[256,128]{1,0:T(8,128)(2,1)S(1)} all-gather(bf16[64,128]{1,0:T(8,128)(2,1)S(1)} %get-tuple-element.762), channel_id=2, replica_groups=mesh['groups'=2,'feat'=4,'layer'=2,'tok'=2] {'feat'}, dimensions={0}, use_global_device_ids=true | all-gather | bytes 81920 | tf_op jit(solution)/shard_map/while/body/eval_jaxpr/all_gather | solution.py:125
  171.9 1.6 fusion.63
  173.5 5.1 %collective-permute-start.1 = (f32[2,64,448]{2,1,0:T(8,128)S(1)}, f32[2,64,448]{2,1,0:T(8,128)}, u32[]{:S(2)}, u32[]{:S(2)}) collective-permute-start(f32[2,64,448]{2,1,0:T(8,128)S(1)} %fusion.63), channel_id=1, source_target_pairs={{0,2},{1,3},{4,6},{5,7},{8,10},{9,11},{12,14},{13,15},{16,18},{17,... | collective-permute-start | bytes 688136 | tf_op jit(solution)/shard_map/while/body/eval_jaxpr/ppermute | solution.py:10
  178.6 1.7 select_dynamic-update-slice_fusion.5
  180.2 1.3 collective-permute-start
  181.5 3.0 %collective-permute-done = f32[64,448]{1,0:T(8,128)S(1)} collective-permute-done((f32[64,448]{1,0:T(8,128)S(1)}, f32[64,448]{1,0:T(8,128)S(1)}, u32[]{:S(2)}, u32[]{:S(2)}) %collective-permute-start) | collective-permute-done | bytes 114720 | tf_op jit(solution)/shard_map/while/body/eval_jaxpr/ppermute | solution.py:10
  184.7 14.4 %all-gather.9 = bf16[4,448,64]{1,2,0:T(8,128)(2,1)S(1)} all-gather(bf16[1,448,64]{1,2,0:T(8,128)(2,1)S(1)} %fusion.57), channel_id=1, replica_groups=mesh['groups'=2,'feat'=4,'layer'=2,'tok'=2] {'feat'}, dimensions={0}, use_global_device_ids=true | all-gather | bytes 286720 | tf_op jit(solution)/shard_map/while/body/eval_jaxpr/all_gather | solution.py:14
  199.4 0.3 reshape.113
  199.6 1.5 fusion.58
  201.1 3.6 %psum.34 = bf16[64,256]{1,0:T(8,128)(2,1)S(1)} all-reduce(f32[64,256]{1,0:T(8,128)S(1)} %fusion.58), channel_id=1, replica_groups=mesh['groups'=2,'feat'=4,'layer'=2,'tok'=2] {'tok'}, use_global_device_ids=true, to_apply=%region_2.2 | all-reduce | flops 16384 | bytes 98304 | tf_op jit(solution)/shard_map/while/body/eval_jaxpr/psum | solution.py:18
  204.7 0.7 dynamic_slice.163
  205.4 0.7 iota_compare_fusion.4
  206.4 15.6 %all_gather.57 = bf16[64,2048]{0,1:T(8,128)(2,1)S(1)} all-gather(bf16[64,512]{0,1:T(8,128)(2,1)S(1)} %bitcast.104), channel_id=1, replica_groups=mesh['groups'=2,'feat'=4,'layer'=2,'tok'=2] {'feat'}, dimensions={1}, use_global_device_ids=true | all-gather | bytes 327680 | tf_op jit(solution)/shard_map/while/body/eval_jaxpr/all_gather | solution.py:113
  222.0 0.5 convolution_add_fusion.2
  222.6 14.5 %all-gather.10 = bf16[4,448,64]{1,2,0:T(8,128)(2,1)S(1)} all-gather(bf16[1,448,64]{1,2,0:T(8,128)(2,1)S(1)} %fusion.61), channel_id=1, replica_groups=mesh['groups'=2,'feat'=4,'layer'=2,'tok'=2] {'feat'}, dimensions={0}, use_global_device_ids=true | all-gather | bytes 286720 | tf_op jit(solution)/shard_map/while/body/eval_jaxpr/all_gather | solution.py:14
  237.3 0.3 reshape.114
  237.6 1.2 fusion.62
  238.8 3.4 %psum.35 = f32[64,128]{1,0:T(8,128)S(1)} all-reduce(f32[64,128]{1,0:T(8,128)S(1)} %fusion.62), channel_id=1, replica_groups=mesh['groups'=2,'feat'=4,'layer'=2,'tok'=2] {'tok'}, use_global_device_ids=true, to_apply=%region_3.3 | all-reduce | flops 8192 | bytes 65536 | tf_op jit(solution)/shard_map/while/body/eval_jaxpr/psum | solution.py:18
  242.3 13.1 %all-gather.11 = bf16[256,128]{1,0:T(8,128)(2,1)S(1)} all-gather(bf16[64,128]{1,0:T(8,128)(2,1)S(1)} %get-tuple-element.762), channel_id=2, replica_groups=mesh['groups'=2,'feat'=4,'layer'=2,'tok'=2] {'feat'}, dimensions={0}, use_global_device_ids=true | all-gather | bytes 81920 | tf_op jit(solution)/shard_map/while/body/eval_jaxpr/all_gather | solution.py:125
  255.6 1.6 fusion.63
  257.1 5.1 %collective-permute-start.1 = (f32[2,64,448]{2,1,0:T(8,128)S(1)}, f32[2,64,448]{2,1,0:T(8,128)}, u32[]{:S(2)}, u32[]{:S(2)}) collective-permute-start(f32[2,64,448]{2,1,0:T(8,128)S(1)} %fusion.63), channel_id=1, source_target_pairs={{0,2},{1,3},{4,6},{5,7},{8,10},{9,11},{12,14},{13,15},{16,18},{17,... | collective-permute-start | bytes 688136 | tf_op jit(solution)/shard_map/while/body/eval_jaxpr/ppermute | solution.py:10
  262.3 1.7 select_dynamic-update-slice_fusion.5
  263.9 1.3 collective-permute-start
  265.2 3.0 %collective-permute-done = f32[64,448]{1,0:T(8,128)S(1)} collective-permute-done((f32[64,448]{1,0:T(8,128)S(1)}, f32[64,448]{1,0:T(8,128)S(1)}, u32[]{:S(2)}, u32[]{:S(2)}) %collective-permute-start) | collective-permute-done | bytes 114720 | tf_op jit(solution)/shard_map/while/body/eval_jaxpr/ppermute | solution.py:10
  268.3 1.8 copy.49
  (61 shorter events, 3.8 us)
Async XLA Ops:
  0.6 1.0 copy-start
  9.8 3.5 %copy-start.2 = (f32[128,1,448]{0,2,1:T(8,128)S(1)}, f32[128,1,448]{0,2,1:T(8,128)}, u32[]{:S(2)}) copy-start(f32[128,1,448]{0,2,1:T(8,128)} %param.17) | copy-start | bytes 688132
  9.8 3.7 %copy-start.3 = (f32[1,128,1,448]{1,3,2,0:T(8,128)S(1)}, f32[1,128,1,448]{1,3,2,0:T(8,128)}, u32[]{:S(2)}) copy-start(f32[1,128,1,448]{1,3,2,0:T(8,128)} %param.27) | copy-start | bytes 688132
  9.8 6.0 %copy-start.4 = (f32[1,128]{1,0:T(1,128)S(1)}, f32[1,128]{1,0:T(1,128)}, u32[]{:S(2)}) copy-start(f32[1,128]{1,0:T(1,128)} %param.25) | copy-start | bytes 1540
  9.8 6.0 %copy-start.5 = (f32[1,128]{1,0:T(1,128)S(1)}, f32[1,128]{1,0:T(1,128)}, u32[]{:S(2)}) copy-start(f32[1,128]{1,0:T(1,128)} %param.18) | copy-start | bytes 1540
  9.9 6.0 %copy-start.6 = (s32[2]{0:T(128)S(1)}, s32[2]{0:T(128)}, u32[]{:S(2)}) copy-start(s32[2]{0:T(128)} %param.21) | copy-start | bytes 28
  9.9 6.0 %copy-start.7 = (f32[1,128]{1,0:T(1,128)S(1)}, f32[1,128]{1,0:T(1,128)}, u32[]{:S(2)}) copy-start(f32[1,128]{1,0:T(1,128)} %param.19) | copy-start | bytes 1540
  90.8 10.1 %collective-permute-start.1 = (f32[2,64,448]{2,1,0:T(8,128)S(1)}, f32[2,64,448]{2,1,0:T(8,128)}, u32[]{:S(2)}, u32[]{:S(2)}) collective-permute-start(f32[2,64,448]{2,1,0:T(8,128)S(1)} %fusion.63), channel_id=1, source_target_pairs={{0,2},{1,3},{4,6},{5,7},{8,10},{9,11},{12,14},{13,15},{16,18},{17,... | collective-permute-start | bytes 688136 | tf_op jit(solution)/shard_map/while/body/eval_jaxpr/ppermute | solution.py:10
  96.5 4.3 %collective-permute-start = (f32[64,448]{1,0:T(8,128)S(1)}, f32[64,448]{1,0:T(8,128)S(1)}, u32[]{:S(2)}, u32[]{:S(2)}) collective-permute-start(f32[64,448]{1,0:T(8,128)S(1)} %get-tuple-element.763), channel_id=1, source_target_pairs={{0,2},{1,3},{4,6},{5,7},{8,10},{9,11},{12,14},{13,15},{16,18},{17,... | collective-permute-start | bytes 344072 | tf_op jit(solution)/shard_map/while/body/eval_jaxpr/ppermute | solution.py:10
  173.5 11.1 %collective-permute-start.1 = (f32[2,64,448]{2,1,0:T(8,128)S(1)}, f32[2,64,448]{2,1,0:T(8,128)}, u32[]{:S(2)}, u32[]{:S(2)}) collective-permute-start(f32[2,64,448]{2,1,0:T(8,128)S(1)} %fusion.63), channel_id=1, source_target_pairs={{0,2},{1,3},{4,6},{5,7},{8,10},{9,11},{12,14},{13,15},{16,18},{17,... | collective-permute-start | bytes 688136 | tf_op jit(solution)/shard_map/while/body/eval_jaxpr/ppermute | solution.py:10
  180.2 4.3 %collective-permute-start = (f32[64,448]{1,0:T(8,128)S(1)}, f32[64,448]{1,0:T(8,128)S(1)}, u32[]{:S(2)}, u32[]{:S(2)}) collective-permute-start(f32[64,448]{1,0:T(8,128)S(1)} %get-tuple-element.763), channel_id=1, source_target_pairs={{0,2},{1,3},{4,6},{5,7},{8,10},{9,11},{12,14},{13,15},{16,18},{17,... | collective-permute-start | bytes 344072 | tf_op jit(solution)/shard_map/while/body/eval_jaxpr/ppermute | solution.py:10
  257.1 11.1 %collective-permute-start.1 = (f32[2,64,448]{2,1,0:T(8,128)S(1)}, f32[2,64,448]{2,1,0:T(8,128)}, u32[]{:S(2)}, u32[]{:S(2)}) collective-permute-start(f32[2,64,448]{2,1,0:T(8,128)S(1)} %fusion.63), channel_id=1, source_target_pairs={{0,2},{1,3},{4,6},{5,7},{8,10},{9,11},{12,14},{13,15},{16,18},{17,... | collective-permute-start | bytes 688136 | tf_op jit(solution)/shard_map/while/body/eval_jaxpr/ppermute | solution.py:10
  263.9 4.3 %collective-permute-start = (f32[64,448]{1,0:T(8,128)S(1)}, f32[64,448]{1,0:T(8,128)S(1)}, u32[]{:S(2)}, u32[]{:S(2)}) collective-permute-start(f32[64,448]{1,0:T(8,128)S(1)} %get-tuple-element.763), channel_id=1, source_target_pairs={{0,2},{1,3},{4,6},{5,7},{8,10},{9,11},{12,14},{13,15},{16,18},{17,... | collective-permute-start | bytes 344072 | tf_op jit(solution)/shard_map/while/body/eval_jaxpr/ppermute | solution.py:10
  268.3 1.8 copy-start.1
